TPU v7x, 32 devices: a whole 2x2x4 slice. The times are simulated.
32 devices in a mesh: grp: 2 (over y), slc: 4 (over z), coil: 2 (over x), vol: 2 (over core).
Axes of the slice: x: 2, y: 2, z: 4, core: 2. Of those that a mesh axis runs over, the one named last changes fastest.
Arguments:
- images: bfloat16 [4, 32, 2, 220, 220], P(('grp', 'vol'), 'slc'), parts along dimension 0, may hold values from -6 to 6
- coil_maps: bfloat16 [8, 32, 2, 220, 220], P(('grp', 'coil'), 'slc'), parts along dimension 0, may hold values from -3 to 3
- kspace: bfloat16 [4, 4, 4, 2, 220, 220], P(('grp', 'vol'), 'slc', 'coil'), parts along dimension 0, may hold values from -12 to 12
- shift_index: int32 [32], P('slc'), may hold values from 0 to 7
- phase_offset: float32 [32, 220], P('slc'), may hold values from -3.140625 to 3.140625
- group_order: int32 [4], replicated, may hold values from 0 to 3, each once
Outputs:
- grad_phase: float32 [64, 220], P(('grp', 'slc')), parts along dimension 0
There are 2 independent parts, one for each index of `grp`. A program takes and returns all parts, laid end to end along the dimension named above; an argument that names none is the same for every part. Nothing has to cross between parts.
Inputs may be any that keep to these rules, and one draw needn't show every extreme that they name: group_order names each of the 4 measured rows exactly once.
All inputs are finite; a program needn't handle non-finite values.
Results may differ from a plain program's by a relative error of at most 0.0096.
Values may be sent and summed in bfloat16 or wider, within the bound.
A program may use at most 64 MiB of HBM per device.

v0:
```python
import math

import jax
import jax.numpy as jnp
from jax import lax
from jax.sharding import PartitionSpec as P

MB = 8


def fourier_tables(length):
    positions = jnp.arange(length, dtype=jnp.int32)
    product = positions[:, None] * positions[None, :] % length
    radians = 2.0 * math.pi / length * product.astype(jnp.float32)
    factor = 1.0 / math.sqrt(length)
    return (
        (jnp.cos(radians) * factor).astype(jnp.bfloat16),
        (-jnp.sin(radians) * factor).astype(jnp.bfloat16),
    )


def slice_phases(shift_index, phase_offset, length):
    lines = (jnp.arange(length, dtype=jnp.int32) - length // 2).astype(jnp.float32)
    return (
        2.0 * math.pi / MB * (shift_index.astype(jnp.float32)[:, None] * lines[None, :])
        + phase_offset
    )


def body(images, coil_maps, kspace, shift_index, phase_offset, group_order):
    per_device = images.shape[1]
    matrix = images.shape[-1]
    groups = lax.axis_size("slc")
    spread = max(1, per_device // groups)
    slot_count = groups * spread
    cos_table, sin_table = fourier_tables(matrix)
    section_one = jnp.stack([jnp.stack([cos_table, -sin_table]), jnp.stack([sin_table, cos_table])])
    section_two = jnp.stack([jnp.stack([cos_table, sin_table]), jnp.stack([-sin_table, cos_table])])
    image_re = images[:, None, :, 0].astype(jnp.float32)
    image_im = images[:, None, :, 1].astype(jnp.float32)
    map_re = coil_maps[None, :, :, 0].astype(jnp.float32)
    map_im = coil_maps[None, :, :, 1].astype(jnp.float32)
    coil_image = jnp.stack(
        [map_re * image_re - map_im * image_im, map_re * image_im + map_im * image_re], axis=3
    ).astype(jnp.bfloat16)
    partly = jnp.einsum(
        "pqky,tcsqyx->tcspkx", section_one, coil_image, preferred_element_type=jnp.float32
    ).astype(jnp.bfloat16)
    spectra = jnp.einsum(
        "tcsqyx,qpkx->tcspyk", partly, section_two, preferred_element_type=jnp.float32
    )
    phase_angle = slice_phases(shift_index, phase_offset, matrix)
    cosine = jnp.cos(phase_angle)[None, None, :, :, None]
    sine = jnp.sin(phase_angle)[None, None, :, :, None]
    spec_re = spectra[:, :, :, 0]
    spec_im = spectra[:, :, :, 1]
    shifted = jnp.stack(
        [spec_re * cosine - spec_im * sine, spec_re * sine + spec_im * cosine], axis=3
    ).astype(jnp.bfloat16)
    position = lax.axis_index("slc")
    within = jnp.arange(per_device, dtype=jnp.int32)
    classes = (position * per_device + within) % groups
    class_match = (classes[:, None] == jnp.arange(groups, dtype=jnp.int32)[None, :]).astype(
        jnp.int32
    )
    target = jnp.sum(class_match * group_order[None, :], axis=1)
    slot_index = target * spread + within // groups
    onehot = (jnp.arange(slot_count, dtype=jnp.int32)[:, None] == slot_index[None, :]).astype(
        jnp.int32
    )
    source = jnp.sum(onehot * within[None, :], axis=1)
    filled = jnp.sum(onehot, axis=1)
    outgoing = jnp.take(shifted, source, axis=2)
    outgoing = jnp.where(
        filled[None, None, :, None, None, None] > 0, outgoing, jnp.zeros_like(outgoing)
    )
    incoming = lax.all_to_all(outgoing, "slc", split_axis=2, concat_axis=2, tiled=True)
    aliased = jnp.sum(incoming, axis=2, dtype=jnp.float32)
    residual = (aliased - kspace[:, 0].astype(jnp.float32)).astype(jnp.bfloat16)
    partial_value = jnp.einsum(
        "tcpyx,tcyx->py",
        incoming[:, :, :, 0],
        residual[:, :, 1],
        preferred_element_type=jnp.float32,
    )
    partial_value = partial_value - jnp.einsum(
        "tcpyx,tcyx->py",
        incoming[:, :, :, 1],
        residual[:, :, 0],
        preferred_element_type=jnp.float32,
    )
    returned = lax.all_to_all(partial_value, "slc", split_axis=0, concat_axis=0, tiled=True)
    local_grad = jnp.dot(onehot.T.astype(jnp.float32), returned, precision=lax.Precision.HIGHEST)
    summed = lax.psum(local_grad, "coil")
    summed = lax.psum(summed, "vol")
    factor = 1.0 / (
        coil_maps.shape[0] * lax.axis_size("coil") * images.shape[0] * lax.axis_size("vol")
    )
    return summed * factor


def solution(mesh):
    placed = (
        P(("grp", "vol"), "slc", None, None, None),
        P(("grp", "coil"), "slc", None, None, None),
        P(("grp", "vol"), "slc", "coil", None, None, None),
        P("slc"),
        P("slc", None),
        P(),
    )
    return jax.shard_map(
        body, mesh=mesh, in_specs=placed, out_specs=P(("grp", "slc"), None), check_vma=False
    )
```

profile of v0, /device:TPU:0, one launch (start us, length us, event | category | flops | bytes accessed | tf_op | source)
XLA Modules:
  0.0 203.3 jit_solution(2907559436263162743)
XLA Ops:
  0.0 1.0 multiply_convert_fusion
  1.0 0.9 fusion.37
  2.0 13.7 %fusion.50 = (bf16[2,8,1,220,220]{4,2,3,1,0:T(2,128)(2,1)}, bf16[2,8,1,220,220]{4,2,3,1,0:T(2,128)(2,1)}) fusion(bf16[2,8,2,220,220]{4,2,3,1,0:T(2,128)(2,1)} %param.7), kind=kLoop, calls=%fused_computation.93 | loop fusion | bytes 6195200 | tf_op jit(solution)/shard_map/slice | solution.py:42
  15.6 8.6 %copy.97 = bf16[2,8,1,220,220]{3,4,2,1,0:T(8,128)(2,1)} copy(bf16[2,8,1,220,220]{4,2,3,1,0:T(2,128)(2,1)} %get-tuple-element.14) | data formatting | bytes 3097600
  24.2 8.7 %copy.99 = bf16[2,8,1,220,220]{3,4,2,1,0:T(8,128)(2,1)} copy(bf16[2,8,1,220,220]{4,2,3,1,0:T(2,128)(2,1)} %get-tuple-element.13) | data formatting | bytes 3097600
  32.9 2.5 %fusion.51 = (bf16[1,8,1,220,220]{4,2,3,1,0:T(2,128)(2,1)S(1)}, bf16[1,8,1,220,220]{4,2,3,1,0:T(2,128)(2,1)S(1)}) fusion(bf16[1,8,2,220,220]{4,2,3,1,0:T(2,128)(2,1)S(1)} %copy-done), kind=kLoop, calls=%fused_computation.94 | loop fusion | bytes 3097600 | tf_op jit(solution)/shard_map/slice | solution.py:39
  35.4 2.4 %fusion.19 = (f32[8,220,220]{2,0,1:T(8,128)}, f32[8,220,220]{2,0,1:T(8,128)}) fusion(bf16[1,8,1,220,220]{4,2,3,1,0:T(2,128)(2,1)S(1)} %get-tuple-element.16, bf16[1,8,1,220,220]{4,2,3,1,0:T(2,128)(2,1)S(1)} %get-tuple-element.15), kind=kLoop, calls=%fused_computation.32 | loop fusion | flops 774400 | bytes 4646400 | tf_op jit(solution)/shard_map/convert_element_type | solution.py:40
  37.8 2.1 %copy.70 = f32[8,220,220]{1,2,0:T(8,128)S(1)} copy(f32[8,220,220]{2,0,1:T(8,128)} %get-tuple-element.27) | data formatting | bytes 3097600 | tf_op jit(solution)/shard_map/convert_element_type | solution.py:40
  39.9 2.8 %copy.67 = f32[8,220,220]{1,2,0:T(8,128)} copy(f32[8,220,220]{2,0,1:T(8,128)} %get-tuple-element.28) | data formatting | bytes 3097600 | tf_op jit(solution)/shard_map/convert_element_type | solution.py:39
  42.8 0.1 convert_reduce_fusion.1
  43.2 5.7 %fusion.1 = (bf16[2,8,1,220,220]{3,4,2,1,0:T(8,128)(2,1)}, bf16[2,8,1,220,220]{3,4,2,1,0:T(8,128)(2,1)}) fusion(bf16[2,8,1,220,220]{3,4,2,1,0:T(8,128)(2,1)} %copy.97, bf16[2,8,1,220,220]{3,4,2,1,0:T(8,128)(2,1)} %copy.99, f32[8,220,220]{1,2,0:T(8,128)S(1)} %copy.70, f32[8,220,220]{1,2,0:T(8,128)} %copy.67), kind=kLoop, calls=%fused_computation.8 | loop fusion | flops 7744000 | bytes 9292800 | tf_op jit(solution)/shard_map/convert.5
  49.0 9.0 %fusion.11 = f32[1,2,8,2,220,220]{4,5,2,1,3,0:T(8,128)} fusion(bf16[2,8,1,220,220]{3,4,2,1,0:T(8,128)(2,1)} %get-tuple-element.10, bf16[2,8,1,220,220]{3,4,2,1,0:T(8,128)(2,1)} %get-tuple-element.9, bf16[1,2,220,220]{3,2,1,0:T(8,128)(2,1)S(1)} %get-tuple-element.20, bf16[1,2,220,220]{3,2,1,0:T(8,128)(2,1)S(1)} %get-tuple-element.23, ...), kind=kOutput, calls=%fused_computation.22 | convolution fusion | flops 2734599936 | bytes 10067200 | tf_op jit(solution)/shard_map/tcsqyx,qpkx->tcspyk/dot_general | solution.py:49
  58.0 4.3 %subtract_convert_fusion = (bf16[1,2,8,1,220,220]{4,5,2,1,3,0:T(8,128)(2,1)S(1)}, bf16[1,2,8,1,220,220]{4,5,2,1,3,0:T(8,128)(2,1)S(1)}) fusion(f32[1,2,8,2,220,220]{4,5,2,1,3,0:T(8,128)} %fusion.11, f32[8,220]{1,0:T(8,128)S(1)} %get-tuple-element.26, f32[8,220]{1,0:T(8,128)S(1)} %get-tuple-element.25), kind=kLoop, calls=%fused_computation.21 | loop fusion | flops 6195200 | bytes 9306880 | tf_op jit(solution)/shard_map/convert.3
  62.3 2.5 %maximum_bitcast_fusion.2 = bf16[2,8,2,220,220]{3,4,1,0,2:T(8,128)(2,1)} fusion(bf16[1,2,8,1,220,220]{4,5,2,1,3,0:T(8,128)(2,1)S(1)} %get-tuple-element.8, bf16[1,2,8,1,220,220]{4,5,2,1,3,0:T(8,128)(2,1)S(1)} %get-tuple-element.7), kind=kLoop, calls=%fused_computation.17 | loop fusion | flops 1548800 | bytes 6195200 | tf_op jit(solution)/shard_map/stack | solution.py:57
  64.8 4.7 %gather_fusion = bf16[8,2,2,220,220]{3,4,1,2,0:T(8,128)(2,1)} fusion(bf16[2,8,2,220,220]{3,4,1,0,2:T(8,128)(2,1)} %maximum_bitcast_fusion.2, s32[1024]{0:T(1024)S(1)} %pad_clamp_fusion), kind=kCustom, calls=%fused_computation | custom fusion | bytes 6195232 | tf_op jit(solution)/shard_map/jit(_take)/gather | solution.py:73
  69.5 4.3 %fusion.10 = bf16[1,2,8,2,220,220]{4,5,1,3,2,0:T(8,128)(2,1)} fusion(bf16[8,2,2,220,220]{3,4,1,2,0:T(8,128)(2,1)} %gather_fusion, pred[8]{0:T(512)(128)(4,1)S(1)} %get-tuple-element.31, pred[8]{0:T(512)(128)(4,1)S(1)} %get-tuple-element.32), kind=kLoop, calls=%fused_computation.19 | loop fusion | flops 3097600 | bytes 6195216 | tf_op jit(solution)/shard_map/jit(_where)/select_n | solution.py:74
  73.8 11.0 %copy.73 = bf16[1,2,8,2,220,220]{5,3,4,1,0,2:T(2,128)(2,1)} copy(bf16[1,2,8,2,220,220]{4,5,1,3,2,0:T(8,128)(2,1)} %fusion.10) | data formatting | bytes 6195200 | tf_op jit(solution)/shard_map/jit(_where)/select_n | solution.py:74
  84.8 6.5 %all-to-all-start = ((bf16[1,2,8,2,220,220]{5,3,4,1,0,2:T(2,128)(2,1)}), bf16[1,2,8,2,220,220]{5,3,4,1,0,2:T(2,128)(2,1)}, u32[]{:S(2)}, u32[]{:S(2)}) async-start(bf16[1,2,8,2,220,220]{5,3,4,1,0,2:T(2,128)(2,1)} %copy.73), calls=%async_computation | async-start | bytes 7208960 | tf_op jit(solution)/shard_map/all_to_all | solution.py:77
  91.3 0.4 copy.76
  91.7 80.5 %all-to-all-done = bf16[1,2,8,2,220,220]{5,3,4,1,0,2:T(2,128)(2,1)} async-done(((bf16[1,2,8,2,220,220]{5,3,4,1,0,2:T(2,128)(2,1)}), bf16[1,2,8,2,220,220]{5,3,4,1,0,2:T(2,128)(2,1)}, u32[]{:S(2)}, u32[]{:S(2)}) %all-to-all-start) | async-done | bytes 3097632 | tf_op jit(solution)/shard_map/all_to_all | solution.py:77
  172.2 3.3 %copy.74 = bf16[1,2,8,2,220,220]{5,2,4,3,1,0:T(8,128)(2,1)S(1)} copy(bf16[1,2,8,2,220,220]{5,3,4,1,0,2:T(2,128)(2,1)} %all-to-all-done) | data formatting | bytes 6195200 | tf_op jit(solution)/shard_map/all_to_all | solution.py:77
  175.5 2.0 %slice_bitcast_fusion.1 = (bf16[2,8,220,220]{3,1,2,0:T(8,128)(2,1)}, bf16[2,8,220,220]{3,1,2,0:T(8,128)(2,1)}) fusion(bf16[1,2,8,2,220,220]{5,2,4,3,1,0:T(8,128)(2,1)S(1)} %copy.74), kind=kLoop, calls=%fused_computation.24 | loop fusion | bytes 6195200 | tf_op jit(solution)/shard_map/reshape.15
  177.5 5.2 %convert_reduce_fusion = f32[2,2,220,220]{3,2,1,0:T(8,128)S(1)} fusion(bf16[1,2,8,2,220,220]{5,3,4,1,0,2:T(2,128)(2,1)} %all-to-all-done), kind=kLoop, calls=%fused_computation.2 | loop fusion | flops 2904000 | bytes 3872000 | tf_op jit(solution)/shard_map/reduce_sum | solution.py:78
  182.7 0.3 copy.96
  183.3 2.4 %fusion.14 = f32[220,1,8,1]{2,1,3,0:T(1,128)S(1)} fusion(bf16[2,8,220,220]{3,1,2,0:T(8,128)(2,1)} %get-tuple-element.12, bf16[2,220,220,1]{2,1,0,3:T(8,128)(2,1)S(1)} %bitcast.99), kind=kOutput, calls=%fused_computation.25 | convolution fusion | flops 1548800 | bytes 1749440 | tf_op jit(solution)/shard_map/tcpyx,tcyx->py/dot_general | solution.py:86
  185.8 0.1 copy.77
  186.0 0.9 fusion.16
  187.0 8.0 %all_to_all.17 = f32[4,2,220]{2,1,0:T(2,128)S(1)} all-to-all(f32[4,2,220]{2,1,0:T(2,128)S(1)} %all_to_all.12), channel_id=1, replica_groups=mesh['grp'=2,'slc'=4,'coil'=2,'vol'=2] {'slc'}, dimensions={0} | all-to-all | bytes 14080 | tf_op jit(solution)/shard_map/all_to_all | solution.py:92
  195.0 0.2 fusion.41
  195.2 5.0 %psum.14 = f32[8,220]{1,0:T(8,128)S(1)} all-reduce(f32[8,220]{1,0:T(8,128)S(1)} %fusion.41), channel_id=1, replica_groups=mesh['grp'=2,'slc'=4,'coil'=2,'vol'=2] {'coil'}, use_global_device_ids=true, to_apply=%region_4.5 | all-reduce | flops 1760 | bytes 14080 | tf_op jit(solution)/shard_map/psum | solution.py:94
  200.2 2.5 %psum.15 = f32[8,220]{1,0:T(8,128)S(1)} all-reduce(f32[8,220]{1,0:T(8,128)S(1)} %psum.14), channel_id=1, replica_groups=mesh['grp'=2,'slc'=4,'coil'=2,'vol'=2] {'vol'}, use_global_device_ids=true, to_apply=%region_5.6 | all-reduce | flops 1760 | bytes 14080 | tf_op jit(solution)/shard_map/psum | solution.py:95
  202.7 0.6 broadcast_multiply_fusion
  (30 shorter events, 0.8 us)
Async XLA Ops:
  24.2 8.7 %copy-start = (bf16[1,8,2,220,220]{4,2,3,1,0:T(2,128)(2,1)S(1)}, bf16[1,8,2,220,220]{4,2,3,1,0:T(2,128)(2,1)}, u32[]{:S(2)}) copy-start(bf16[1,8,2,220,220]{4,2,3,1,0:T(2,128)(2,1)} %param.6) | copy-start | bytes 4646404
  37.8 4.9 %copy-start.4 = (s32[8]{0:T(128)S(1)}, s32[8]{0:T(128)}, u32[]{:S(2)}) copy-start(s32[8]{0:T(128)} %param.9) | copy-start | bytes 100
  37.8 4.9 %copy-start.5 = (s32[4]{0:T(128)S(1)}, s32[4]{0:T(128)}, u32[]{:S(2)}) copy-start(s32[4]{0:T(128)} %param.11) | copy-start | bytes 52
  37.8 5.3 %copy-start.3 = (f32[8,220]{1,0:T(8,128)S(1)}, f32[8,220]{1,0:T(8,128)}, u32[]{:S(2)}) copy-start(f32[8,220]{1,0:T(8,128)} %param.10) | copy-start | bytes 21124
  84.8 6.5 %copy-start.2 = (bf16[1,1,2,2,220,220]{5,3,4,2,1,0:T(2,128)(2,1)S(1)}, bf16[1,1,2,2,220,220]{5,3,4,2,1,0:T(2,128)(2,1)}, u32[]{:S(2)}) copy-start(bf16[1,1,2,2,220,220]{5,3,4,2,1,0:T(2,128)(2,1)} %param.8) | copy-start | bytes 1161604
  84.8 87.4 %all-to-all-start = ((bf16[1,2,8,2,220,220]{5,3,4,1,0,2:T(2,128)(2,1)}), bf16[1,2,8,2,220,220]{5,3,4,1,0,2:T(2,128)(2,1)}, u32[]{:S(2)}, u32[]{:S(2)}) async-start(bf16[1,2,8,2,220,220]{5,3,4,1,0,2:T(2,128)(2,1)} %copy.73), calls=%async_computation | async-start | bytes 7208960 | tf_op jit(solution)/shard_map/all_to_all | solution.py:77
  183.1 2.9 %copy-start.1 = (bf16[2,8,220,220]{3,1,2,0:T(8,128)(2,1)S(1)}, bf16[2,8,220,220]{3,1,2,0:T(8,128)(2,1)}, u32[]{:S(2)}) copy-start(bf16[2,8,220,220]{3,1,2,0:T(8,128)(2,1)} %get-tuple-element.11) | copy-start | bytes 4646404
where the time goes:
time: 204 us; the launch traced here: 203 us
  waiting for transfers between devices  80.5 us (39%)
  local copies, waits for them, and re-layouts  60.6 us (30%)
  other arithmetic  27.6 us (14%)
  blocking collectives  15.5 us (8%)
  matrix products  12.5 us (6%)
  starting transfers between devices  6.47 us (3%)
    all_to_all x1, waiting for transfers between devices, body(): lax.all_to_all(outgoing, 'slc', split_axis=2, concat_axis=2, tiled=True)  80.5 us
    unnamed x16, local copies, waits for them, and re-layouts  18 us
    slice x1, local copies, waits for them, and re-layouts, body(): map_im = coil_maps[None, :, :, 1].astype(jnp.float32)  13.7 us
    select_n x1, local copies, waits for them, and re-layouts, body(): jnp.where(filled[None, None, :, None, None, None] > 0, outgoing, jnp.zero...  11 us
    another operation x2, other arithmetic  10 us
    dot_general x1, matrix products, body(): jnp.einsum('tcsqyx,qpkx->tcspyk', partly, section_two, preferred_element_...  9.01 us
    all_to_all x1, blocking collectives, body(): lax.all_to_all(partial_value, 'slc', split_axis=0, concat_axis=0, tiled=T...  8.04 us
    all_to_all x1, starting transfers between devices, body(): lax.all_to_all(outgoing, 'slc', split_axis=2, concat_axis=2, tiled=True)  6.47 us
  transfers between devices with their start and end apart: 1, of which 1 were waited for; matrix products, arithmetic and copies ran while one was open for 0% of the time, Pallas kernels for 0%

commit v1 on v0

--- a/solution.py
+++ b/solution.py
@@ -1,8 +1,12 @@
+import functools
 import math
 
 import jax
 import jax.numpy as jnp
+import numpy as np
 from jax import lax
+from jax.experimental import pallas as pl
+from jax.experimental.pallas import tpu as pltpu
 from jax.sharding import PartitionSpec as P
 
 MB = 8
@@ -25,6 +29,331 @@
         2.0 * math.pi / MB * (shift_index.astype(jnp.float32)[:, None] * lines[None, :])
         + phase_offset
     )
+
+
+ROWS = 32
+MESH = pl.DeviceIdType.MESH
+F32 = jnp.float32
+BF16 = jnp.bfloat16
+
+
+def round_up(value, unit):
+    return -(-value // unit) * unit
+
+
+def static_tables(length):
+    positions = np.arange(length, dtype=np.int32)
+    product = positions[:, None] * positions[None, :] % length
+    radians = np.float32(2.0 * math.pi / length) * product.astype(np.float32)
+    factor = np.float32(1.0 / math.sqrt(length))
+    cosine = (np.cos(radians) * factor).astype(jnp.bfloat16)
+    sine = (-np.sin(radians) * factor).astype(jnp.bfloat16)
+    return np.asarray(cosine, np.float32), np.asarray(sine, np.float32)
+
+
+def stage_tables(length, coils):
+    cosine, sine = static_tables(length)
+    rows, wide = round_up(length, ROWS), round_up(length, 128)
+    first = np.zeros((3, rows, length), np.float32)
+    first[0, :length], first[1, :length], first[2, :length] = cosine, sine, -sine
+    forward = np.zeros((coils, 2, length, coils * 2 * length), np.float32)
+    back = np.zeros((coils * 2 * length, coils * 2 * wide), np.float32)
+    for coil in range(coils):
+        low = coil * 2 * length
+        mid, top = low + length, low + 2 * length
+        forward[coil, 0, :, low:mid], forward[coil, 0, :, mid:top] = cosine, sine
+        forward[coil, 1, :, low:mid], forward[coil, 1, :, mid:top] = -sine, cosine
+        at = coil * 2 * wide
+        back[low:mid, at : at + length], back[mid:top, at : at + length] = cosine, sine
+        at = at + wide
+        back[low:mid, at : at + length], back[mid:top, at : at + length] = -sine, cosine
+    return first.astype(jnp.bfloat16), forward.astype(jnp.bfloat16), back.astype(jnp.bfloat16)
+
+
+def kernel(
+    sizes,
+    order_ref,
+    trig_ref,
+    images_ref,
+    maps_ref,
+    measured_ref,
+    first_ref,
+    forward_ref,
+    back_ref,
+    out_ref,
+    turned,
+    own,
+    to_right,
+    to_left,
+    from_left,
+    from_right,
+    columns,
+    shares,
+    right_send,
+    left_send,
+    left_recv,
+    right_recv,
+    share_send,
+    share_recv,
+):
+    groups, coil_axis, vol_axis = sizes
+    per_device = images_ref.shape[1]
+    length = images_ref.shape[-1]
+    coils = maps_ref.shape[0]
+    rows, wide = first_ref.shape[1], turned.shape[-1] // (2 * coils)
+    spread = per_device // groups
+    parts = rows // ROWS
+    total = groups * parts
+    spot = lax.axis_index("slc")
+    coil_at, vol_at = lax.axis_index("coil"), lax.axis_index("vol")
+    has_left, has_right = spot > 0, spot < groups - 1
+    peers = coil_axis * vol_axis
+    mine = coil_at * vol_axis + vol_at
+
+    def peer(distance):
+        other = lax.rem(mine + distance, peers)
+        return {"coil": other // vol_axis, "vol": lax.rem(other, vol_axis)}
+
+    barrier = pltpu.get_barrier_semaphore()
+
+    @pl.when(has_left)
+    def _():
+        pl.semaphore_signal(barrier, inc=1, device_id={"slc": spot - 1}, device_id_type=MESH)
+
+    @pl.when(has_right)
+    def _():
+        pl.semaphore_signal(barrier, inc=1, device_id={"slc": spot + 1}, device_id_type=MESH)
+
+    for distance in range(1, peers):
+        pl.semaphore_signal(barrier, inc=1, device_id=peer(distance), device_id_type=MESH)
+
+    def right_copy(chunk):
+        return pltpu.make_async_remote_copy(
+            src_ref=to_right.at[chunk],
+            dst_ref=from_left.at[chunk],
+            send_sem=right_send.at[chunk],
+            recv_sem=left_recv.at[chunk],
+            device_id={"slc": spot + 1},
+            device_id_type=MESH,
+        )
+
+    def left_copy(chunk):
+        return pltpu.make_async_remote_copy(
+            src_ref=to_left.at[chunk],
+            dst_ref=from_right.at[chunk],
+            send_sem=left_send.at[chunk],
+            recv_sem=right_recv.at[chunk],
+            device_id={"slc": spot - 1},
+            device_id_type=MESH,
+        )
+
+    turned[...] = jnp.zeros_like(turned)
+    columns[...] = jnp.zeros_like(columns)
+
+    def dot(left, right):
+        return jnp.dot(left, right, preferred_element_type=F32)
+
+    def compute(group):
+        sums = [[None, None] for _ in range(coils)]
+        for step in range(spread):
+            within = group + step * groups
+            image_re = images_ref[0, within, 0].astype(F32)
+            image_im = images_ref[0, within, 1].astype(F32)
+            cosine = trig_ref[:, 2 * within : 2 * within + 1]
+            sine = trig_ref[:, 2 * within + 1 : 2 * within + 2]
+            for coil in range(coils):
+                map_re = maps_ref[coil, within, 0].astype(F32)
+                map_im = maps_ref[coil, within, 1].astype(F32)
+                coil_re = (map_re * image_re - map_im * image_im).astype(BF16)
+                coil_im = (map_re * image_im + map_im * image_re).astype(BF16)
+                part_re = dot(first_ref[0], coil_re) + dot(first_ref[2], coil_im)
+                part_im = dot(first_ref[0], coil_im) + dot(first_ref[1], coil_re)
+                turn_re = part_re * cosine - part_im * sine
+                turn_im = part_re * sine + part_im * cosine
+                at = coil * 2 * wide
+                turned[within, :, at : at + length] = (-turn_im).astype(BF16)
+                turned[within, :, at + wide : at + wide + length] = turn_re.astype(BF16)
+                for which, value in enumerate((turn_re, turn_im)):
+                    before = sums[coil][which]
+                    sums[coil][which] = value if before is None else before + value
+        spectrum = None
+        for coil in range(coils):
+            for which in range(2):
+                term = dot(sums[coil][which].astype(BF16), forward_ref[coil, which])
+                spectrum = term if spectrum is None else spectrum + term
+        held = jnp.where(order_ref[group] == spot, F32(1.0), F32(0.0))
+        spectrum = spectrum - held * measured_ref[...].astype(F32)
+        own[group * parts : (group + 1) * parts] = spectrum.reshape(parts, ROWS, -1)
+
+        @pl.when(jnp.logical_not(has_left))
+        def _():
+            for chunk in range(group * parts, (group + 1) * parts):
+                to_right[chunk] = own[chunk].astype(BF16)
+                right_copy(chunk).start()
+
+        @pl.when(jnp.logical_not(has_right))
+        def _():
+            for chunk in range(group * parts, (group + 1) * parts):
+                to_left[chunk] = own[chunk].astype(BF16)
+                left_copy(chunk).start()
+
+    late_right = jnp.maximum(0, 2 * spot - (groups - 1))
+    late_left = jnp.maximum(0, (groups - 1) - 2 * spot)
+
+    def wave(tick, carry):
+        chunk = tick - late_right
+
+        @pl.when(has_left & (chunk >= 0) & (chunk < total))
+        def _():
+            right_copy(chunk).wait_recv()
+
+            @pl.when(has_right)
+            def _():
+                to_right[chunk] = (from_left[chunk].astype(F32) + own[chunk]).astype(BF16)
+                right_copy(chunk).start()
+
+        other = tick - late_left
+
+        @pl.when(has_right & (other >= 0) & (other < total))
+        def _():
+            left_copy(other).wait_recv()
+
+            @pl.when(has_left)
+            def _():
+                to_left[other] = (from_right[other].astype(F32) + own[other]).astype(BF16)
+                left_copy(other).start()
+
+        return carry
+
+    def gradient(group):
+        span = pl.ds(group * parts, parts)
+        value = own[span]
+        value = value + jnp.where(has_left, from_left[span].astype(F32), F32(0.0))
+        value = value + jnp.where(has_right, from_right[span].astype(F32), F32(0.0))
+        value = value.reshape(rows, -1).astype(BF16)
+        pulled = dot(value, back_ref[...])
+        for step in range(spread):
+            within = group + step * groups
+            product = pulled * turned[within].astype(F32)
+            columns[0:rows, within : within + 1] = jnp.sum(product, axis=1, keepdims=True)
+
+    def ticks(group):
+        low = 0 if group == 0 else group * parts + groups - 1
+        lax.fori_loop(low, (group + 1) * parts + groups - 1, wave, 0)
+
+    arrivals = has_left.astype(jnp.int32) + has_right.astype(jnp.int32) + (peers - 1)
+    pl.semaphore_wait(barrier, arrivals)
+    compute(0)
+    for group in range(1, groups):
+        compute(group)
+        if group < groups - 1:
+            ticks(group - 1)
+    for group in range(groups):
+        if group >= max(groups - 2, 0):
+            ticks(group)
+        gradient(group)
+
+    shares[mine] = columns[...].T[:per_device]
+
+    def share_copy(distance):
+        return pltpu.make_async_remote_copy(
+            src_ref=shares.at[mine],
+            dst_ref=shares.at[mine],
+            send_sem=share_send.at[distance],
+            recv_sem=share_recv.at[distance],
+            device_id=peer(distance),
+            device_id_type=MESH,
+        )
+
+    for distance in range(1, peers):
+        share_copy(distance).start()
+
+    @pl.when(has_right)
+    def _():
+        def done(chunk, carry):
+            right_copy(chunk).wait_send()
+            return carry
+
+        lax.fori_loop(0, total, done, 0)
+
+    @pl.when(has_left)
+    def _():
+        def done(chunk, carry):
+            left_copy(chunk).wait_send()
+            return carry
+
+        lax.fori_loop(0, total, done, 0)
+
+    for distance in range(1, peers):
+        share_copy(distance).wait()
+    result = shares[0]
+    for other in range(1, peers):
+        result = result + shares[other]
+    out_ref[...] = result[:, :length] * (1.0 / (coils * peers))
+
+
+def fused(images, coil_maps, kspace, shift_index, phase_offset, group_order):
+    per_device, length = images.shape[1], images.shape[-1]
+    coils = coil_maps.shape[0]
+    groups = lax.axis_size("slc")
+    sizes = (groups, lax.axis_size("coil"), lax.axis_size("vol"))
+    peers = sizes[1] * sizes[2]
+    first, forward, back = stage_tables(length, coils)
+    rows, wide = first.shape[1], back.shape[1] // (2 * coils)
+    width = coils * 2 * length
+    angle = slice_phases(shift_index, phase_offset, length)
+    trig = jnp.stack([jnp.cos(angle), jnp.sin(angle)], axis=1).reshape(2 * per_device, length)
+    trig = jnp.pad(trig.T, ((0, rows - length), (0, 0)))
+    measured = jnp.moveaxis(kspace[0, 0], 2, 0).reshape(length, width)
+    measured = jnp.pad(measured, ((0, rows - length), (0, 0)))
+    chunks = groups * rows // ROWS
+    vmem = pl.BlockSpec(memory_space=pltpu.VMEM)
+    smem = pl.BlockSpec(memory_space=pltpu.SMEM)
+    block = pltpu.VMEM((chunks, ROWS, width), BF16)
+    side = pltpu.SemaphoreType.DMA((chunks,))
+    return pl.pallas_call(
+        functools.partial(kernel, sizes),
+        out_shape=jax.ShapeDtypeStruct((per_device, length), F32),
+        in_specs=[smem] + [vmem] * 7,
+        out_specs=vmem,
+        scratch_shapes=[
+            pltpu.VMEM((per_device, rows, coils * 2 * wide), BF16),
+            pltpu.VMEM((chunks, ROWS, width), F32),
+            block,
+            block,
+            block,
+            block,
+            pltpu.VMEM((wide, 128), F32),
+            pltpu.VMEM((peers, per_device, wide), F32),
+            side,
+            side,
+            side,
+            side,
+            pltpu.SemaphoreType.DMA((peers,)),
+            pltpu.SemaphoreType.DMA((peers,)),
+        ],
+        compiler_params=pltpu.CompilerParams(
+            collective_id=0, has_side_effects=True, vmem_limit_bytes=60 * 2**20
+        ),
+    )(
+        group_order,
+        trig,
+        images,
+        coil_maps,
+        measured,
+        jnp.asarray(first),
+        jnp.asarray(forward),
+        jnp.asarray(back),
+    )
+
+
+def program(images, coil_maps, kspace, shift_index, phase_offset, group_order):
+    arguments = (images, coil_maps, kspace, shift_index, phase_offset, group_order)
+    groups = lax.axis_size("slc")
+    even = images.shape[1] % groups == 0 and images.shape[0] == 1 and kspace.shape[1] == 1
+    if even and images.shape[1] <= 128 and groups > 2:
+        return fused(*arguments)
+    return body(*arguments)
 
 
 def body(images, coil_maps, kspace, shift_index, phase_offset, group_order):
@@ -109,5 +438,5 @@
         P(),
     )
     return jax.shard_map(
-        body, mesh=mesh, in_specs=placed, out_specs=P(("grp", "slc"), None), check_vma=False
-    )
+        program, mesh=mesh, in_specs=placed, out_specs=P(("grp", "slc"), None), check_vma=False
+    )

time: 204 us -> 99.8 us (0.49)
  Pallas kernels: 0 us -> 88.1 us
  waiting for transfers between devices: 80.5 us -> 0 us
  local copies, waits for them, and re-layouts: 60.6 us -> 9.72 us
  other arithmetic: 27.6 us -> 1.61 us
  blocking collectives: 15.5 us -> 0 us
  matrix products: 12.5 us -> 0 us
  starting transfers between devices: 6.47 us -> 0 us
    pallas_call x0 -> x1, Pallas kernels: none -> 88.1 us  [fused(): pl.pallas_call(functools.partial(kernel, sizes), out_shape=jax.ShapeDtype...]
    all_to_all x1 -> x0, waiting for transfers between devices: 80.5 us -> none  [body(): lax.all_to_all(outgoing, 'slc', split_axis=2, concat_axis=2, tiled=True)]
    slice x5 -> x0, local copies, waits for them, and re-layouts: 16.5 us -> none  [the longest x1 13.7 us: body(): map_im = coil_maps[None, :, :, 1].astype(jnp.float32)]
    dot_general x4 -> x0, matrix products: 12.5 us -> none  [the longest x1 9.01 us: body(): jnp.einsum('tcsqyx,qpkx->tcspyk', partly, section_two, preferred_element_...]
    another operation x4 -> x2, other arithmetic: 12.6 us -> 0.82 us  [fused(): jnp.stack([jnp.cos(angle), jnp.sin(angle)], axis=1)]
    unnamed x16 -> x7, local copies, waits for them, and re-layouts: 18 us -> 6.43 us
    select_n x1 -> x0, local copies, waits for them, and re-layouts: 11 us -> none  [body(): jnp.where(filled[None, None, :, None, None, None] > 0, outgoing, jnp.zero...]
    all_to_all x1 -> x0, blocking collectives: 8.04 us -> none  [body(): lax.all_to_all(partial_value, 'slc', split_axis=0, concat_axis=0, tiled=T...]
  transfers between devices with their start and end apart: 1 -> 0, of which waited for: 1 -> 0; matrix products, arithmetic and copies ran while one was open for 0% -> 0% of each run, Pallas kernels for 0% -> 0%
where the time goes in v1:
time: 99.8 us; the launch traced here: 99.5 us
  Pallas kernels  88.1 us (88%)
  local copies, waits for them, and re-layouts  9.72 us (10%)
  other arithmetic  1.61 us (2%)
    pallas_call x1, Pallas kernels, fused(): pl.pallas_call(functools.partial(kernel, sizes), out_shape=jax.ShapeDtype...  88.1 us
    unnamed x7, local copies, waits for them, and re-layouts  6.43 us

profile of v1, /device:TPU:0, one launch (start us, length us, event | category | flops | bytes accessed | tf_op | source)
XLA Modules:
  0.0 99.5 jit_solution(1500312491806547009)
XLA Ops:
  0.0 0.0 copy-start.1
  0.0 0.8 convert_element_type.14
  0.8 0.8 cosine_bitcast_fusion
  1.7 0.1 copy.15
  1.8 0.7 pad.8.trig_ref
  2.4 1.3 %copy.16 = bf16[220,2,2,220]{3,2,1,0:T(2,128)(2,1)S(1)} copy(bf16[220,2,2,220]{3,2,0,1:T(2,128)(2,1)} %bitcast.9) | data formatting | bytes 774400 | tf_op jit(solution)/shard_map/transpose | solution.py:307
  3.8 0.3 reshape.13
  4.1 0.8 pad.9.measured_ref
  4.9 0.0 copy-done.1
  4.9 0.0 copy-start
  4.9 1.5 %copy.17.images_ref = bf16[1,8,2,220,220]{4,3,2,1,0:T(8,128)(2,1)} copy(bf16[1,8,2,220,220]{4,2,3,1,0:T(2,128)(2,1)S(1)} %copy-done.1) | data formatting | bytes 3097600 | tf_op args[0]
  6.5 1.1 %copy-done = bf16[2,8,2,220,220]{4,2,3,1,0:T(2,128)(2,1)S(1)} copy-done((bf16[2,8,2,220,220]{4,2,3,1,0:T(2,128)(2,1)S(1)}, bf16[2,8,2,220,220]{4,2,3,1,0:T(2,128)(2,1)}, u32[]{:S(2)}) %copy-start) | copy-done | bytes 3097624
  7.6 2.4 %copy.18.maps_ref = bf16[2,8,2,220,220]{4,3,2,1,0:T(8,128)(2,1)} copy(bf16[2,8,2,220,220]{4,2,3,1,0:T(2,128)(2,1)S(1)} %copy-done) | data formatting | bytes 6195200 | tf_op args[1]
  10.1 88.1 %shard_map.91 = f32[8,220]{1,0:T(8,128)} custom-call(s32[4]{0:T(128)} %order_ref.1, f32[224,16]{1,0:T(8,128)} %pad.8.trig_ref, bf16[1,8,2,220,220]{4,3,2,1,0:T(8,128)(2,1)} %copy.17.images_ref, bf16[2,8,2,220,220]{4,3,2,1,0:T(8,128)(2,1)} %copy.18.maps_ref, bf16[224,880]{1,0:T(8,128)(2,1)} %pad.9.measured_ref, ...), custom_call_target="tpu_custom_call" | custom-call | tf_op jit(solution)/shard_map/pallas_call | solution.py:314
  98.2 1.3 %copy.20 = f32[8,220]{1,0:T(8,128)} copy(f32[8,220]{1,0:T(8,128)} %shard_map.91) | data formatting | bytes 14080
  (4 shorter events, 0.0 us)
Async XLA Ops:
  0.0 4.9 %copy-start.1 = (bf16[1,8,2,220,220]{4,2,3,1,0:T(2,128)(2,1)S(1)}, bf16[1,8,2,220,220]{4,2,3,1,0:T(2,128)(2,1)}, u32[]{:S(2)}) copy-start(bf16[1,8,2,220,220]{4,2,3,1,0:T(2,128)(2,1)} %param.9) | copy-start | bytes 4646404
  4.9 2.7 %copy-start = (bf16[2,8,2,220,220]{4,2,3,1,0:T(2,128)(2,1)S(1)}, bf16[2,8,2,220,220]{4,2,3,1,0:T(2,128)(2,1)}, u32[]{:S(2)}) copy-start(bf16[2,8,2,220,220]{4,2,3,1,0:T(2,128)(2,1)} %param.10) | copy-start | bytes 9292804

commit v2 on v1

--- a/solution.py
+++ b/solution.py
@@ -32,6 +32,7 @@
 
 
 ROWS = 32
+LAG = 3
 MESH = pl.DeviceIdType.MESH
 F32 = jnp.float32
 BF16 = jnp.bfloat16
@@ -197,8 +198,10 @@
                 to_left[chunk] = own[chunk].astype(BF16)
                 left_copy(chunk).start()
 
-    late_right = jnp.maximum(0, 2 * spot - (groups - 1))
-    late_left = jnp.maximum(0, (groups - 1) - 2 * spot)
+    between = jnp.where(has_left & has_right, LAG, 0)
+    late_right = between * jnp.maximum(0, 2 * spot - (groups - 1))
+    late_left = between * jnp.maximum(0, (groups - 1) - 2 * spot)
+    extra = LAG * (groups - 3)
 
     def wave(tick, carry):
         chunk = tick - late_right
@@ -238,8 +241,14 @@
             columns[0:rows, within : within + 1] = jnp.sum(product, axis=1, keepdims=True)
 
     def ticks(group):
-        low = 0 if group == 0 else group * parts + groups - 1
-        lax.fori_loop(low, (group + 1) * parts + groups - 1, wave, 0)
+        low = 0 if group == 0 else group * parts + extra
+        high = (group + 1) * parts + extra
+        end_low = group * parts if group == groups - 1 else 0
+        end_high = (group + 1) * parts if group >= groups - 2 else 0
+        inner = has_left & has_right
+        lax.fori_loop(
+            jnp.where(inner, low, end_low), jnp.where(inner, high, end_high), wave, 0
+        )
 
     arrivals = has_left.astype(jnp.int32) + has_right.astype(jnp.int32) + (peers - 1)
     pl.semaphore_wait(barrier, arrivals)
@@ -248,9 +257,11 @@
         compute(group)
         if group < groups - 1:
             ticks(group - 1)
-    for group in range(groups):
-        if group >= max(groups - 2, 0):
-            ticks(group)
+    ticks(groups - 2)
+    for group in range(groups - 2):
+        gradient(group)
+    ticks(groups - 1)
+    for group in range(groups - 2, groups):
         gradient(group)
 
     shares[mine] = columns[...].T[:per_device]

time: 99.8 us -> 70 us (0.70)
  Pallas kernels: 88.1 us -> 58.4 us
    pallas_call x1, Pallas kernels: 88.1 us -> 58.4 us  [fused(): pl.pallas_call(functools.partial(kernel, sizes), out_shape=jax.ShapeDtype...]
where the time goes in v2:
time: 70 us; the launch traced here: 69.8 us
  Pallas kernels  58.4 us (83%)
  local copies, waits for them, and re-layouts  9.72 us (14%)
  other arithmetic  1.61 us (2%)
    pallas_call x1, Pallas kernels, fused(): pl.pallas_call(functools.partial(kernel, sizes), out_shape=jax.ShapeDtype...  58.4 us
    unnamed x7, local copies, waits for them, and re-layouts  6.43 us

profile of v2, /device:TPU:0, one launch (start us, length us, event | category | flops | bytes accessed | tf_op | source)
XLA Modules:
  0.0 69.8 jit_solution(5334569429915439831)
XLA Ops:
  0.0 0.0 copy-start.1
  0.0 0.8 %convert_element_type.14 = f32[8]{0:T(128)S(1)} convert(s32[8]{0:T(128)} %param.12) | non-fusion elementwise | flops 8 | bytes 64 | tf_op jit(solution)/shard_map/convert_element_type | solution.py:29
  0.8 0.8 %cosine_bitcast_fusion = (f32[8,1,220]{2,0,1:T(8,128)S(1)}, f32[8,1,220]{2,0,1:T(8,128)S(1)}) fusion(f32[8,220]{1,0:T(8,128)} %param.13, f32[220]{0:T(256)S(1)} %add_convert_fusion, f32[8]{0:T(128)S(1)} %convert_element_type.14), kind=kLoop, calls=%fused_computation.2 | loop fusion | flops 5280 | bytes 22032 | tf_op jit(solution)/shard_map/stack | solution.py:316
  1.7 0.1 copy.15
  1.8 0.7 pad.8.trig_ref
  2.4 1.3 %copy.16 = bf16[220,2,2,220]{3,2,1,0:T(2,128)(2,1)S(1)} copy(bf16[220,2,2,220]{3,2,0,1:T(2,128)(2,1)} %bitcast.9) | data formatting | bytes 774400 | tf_op jit(solution)/shard_map/transpose | solution.py:318
  3.8 0.3 reshape.13
  4.1 0.8 %pad.9.measured_ref = bf16[224,880]{1,0:T(8,128)(2,1)} pad(bf16[220,880]{1,0:T(8,128)(2,1)S(1)} %reshape.13, bf16[]{:T(256)} %constant.15.clone.1), padding=0_4x0_0 | pad | bytes 781442 | tf_op jit(solution)/shard_map/jit(_pad)/pad | solution.py:319
  4.9 0.0 copy-done.1
  4.9 0.0 copy-start
  4.9 1.5 %copy.17.images_ref = bf16[1,8,2,220,220]{4,3,2,1,0:T(8,128)(2,1)} copy(bf16[1,8,2,220,220]{4,2,3,1,0:T(2,128)(2,1)S(1)} %copy-done.1) | data formatting | bytes 3097600 | tf_op args[0]
  6.5 1.1 %copy-done = bf16[2,8,2,220,220]{4,2,3,1,0:T(2,128)(2,1)S(1)} copy-done((bf16[2,8,2,220,220]{4,2,3,1,0:T(2,128)(2,1)S(1)}, bf16[2,8,2,220,220]{4,2,3,1,0:T(2,128)(2,1)}, u32[]{:S(2)}) %copy-start) | copy-done | bytes 3097624
  7.6 2.4 %copy.18.maps_ref = bf16[2,8,2,220,220]{4,3,2,1,0:T(8,128)(2,1)} copy(bf16[2,8,2,220,220]{4,2,3,1,0:T(2,128)(2,1)S(1)} %copy-done) | data formatting | bytes 6195200 | tf_op args[1]
  10.1 58.4 %shard_map.91 = f32[8,220]{1,0:T(8,128)} custom-call(s32[4]{0:T(128)} %order_ref.1, f32[224,16]{1,0:T(8,128)} %pad.8.trig_ref, bf16[1,8,2,220,220]{4,3,2,1,0:T(8,128)(2,1)} %copy.17.images_ref, bf16[2,8,2,220,220]{4,3,2,1,0:T(8,128)(2,1)} %copy.18.maps_ref, bf16[224,880]{1,0:T(8,128)(2,1)} %pad.9.measured_ref, ...), custom_call_target="tpu_custom_call" | custom-call | tf_op jit(solution)/shard_map/pallas_call | solution.py:325
  68.5 1.3 %copy.20 = f32[8,220]{1,0:T(8,128)} copy(f32[8,220]{1,0:T(8,128)} %shard_map.91) | data formatting | bytes 14080
  (4 shorter events, 0.0 us)
Async XLA Ops:
  0.0 4.9 %copy-start.1 = (bf16[1,8,2,220,220]{4,2,3,1,0:T(2,128)(2,1)S(1)}, bf16[1,8,2,220,220]{4,2,3,1,0:T(2,128)(2,1)}, u32[]{:S(2)}) copy-start(bf16[1,8,2,220,220]{4,2,3,1,0:T(2,128)(2,1)} %param.9) | copy-start | bytes 4646404
  4.9 2.7 %copy-start = (bf16[2,8,2,220,220]{4,2,3,1,0:T(2,128)(2,1)S(1)}, bf16[2,8,2,220,220]{4,2,3,1,0:T(2,128)(2,1)}, u32[]{:S(2)}) copy-start(bf16[2,8,2,220,220]{4,2,3,1,0:T(2,128)(2,1)} %param.10) | copy-start | bytes 9292804

commit v3 on v2

--- a/solution.py
+++ b/solution.py
@@ -74,10 +74,10 @@
 def kernel(
     sizes,
     order_ref,
-    trig_ref,
+    trig_in,
     images_ref,
     maps_ref,
-    measured_ref,
+    measured_in,
     first_ref,
     forward_ref,
     back_ref,
@@ -89,6 +89,8 @@
     from_left,
     from_right,
     columns,
+    trig_ref,
+    measured_ref,
     shares,
     right_send,
     left_send,
@@ -150,6 +152,10 @@
 
     turned[...] = jnp.zeros_like(turned)
     columns[...] = jnp.zeros_like(columns)
+    trig_ref[...] = jnp.zeros_like(trig_ref)
+    measured_ref[...] = jnp.zeros_like(measured_ref)
+    trig_ref[:length] = trig_in[...]
+    measured_ref[:length] = measured_in[...]
 
     def dot(left, right):
         return jnp.dot(left, right, preferred_element_type=F32)
@@ -160,11 +166,11 @@
             within = group + step * groups
             image_re = images_ref[0, within, 0].astype(F32)
             image_im = images_ref[0, within, 1].astype(F32)
-            cosine = trig_ref[:, 2 * within : 2 * within + 1]
-            sine = trig_ref[:, 2 * within + 1 : 2 * within + 2]
+            cosine = trig_ref[:, within : within + 1]
+            sine = trig_ref[:, per_device + within : per_device + within + 1]
             for coil in range(coils):
-                map_re = maps_ref[coil, within, 0].astype(F32)
-                map_im = maps_ref[coil, within, 1].astype(F32)
+                coil_map = jnp.swapaxes(maps_ref[coil, within].astype(F32), 0, 1)
+                map_re, map_im = coil_map[0], coil_map[1]
                 coil_re = (map_re * image_re - map_im * image_im).astype(BF16)
                 coil_im = (map_re * image_im + map_im * image_re).astype(BF16)
                 part_re = dot(first_ref[0], coil_re) + dot(first_ref[2], coil_im)
@@ -313,10 +319,9 @@
     rows, wide = first.shape[1], back.shape[1] // (2 * coils)
     width = coils * 2 * length
     angle = slice_phases(shift_index, phase_offset, length)
-    trig = jnp.stack([jnp.cos(angle), jnp.sin(angle)], axis=1).reshape(2 * per_device, length)
-    trig = jnp.pad(trig.T, ((0, rows - length), (0, 0)))
+    trig = jnp.concatenate([jnp.cos(angle), jnp.sin(angle)], axis=0)
+    trig = trig.T
     measured = jnp.moveaxis(kspace[0, 0], 2, 0).reshape(length, width)
-    measured = jnp.pad(measured, ((0, rows - length), (0, 0)))
     chunks = groups * rows // ROWS
     vmem = pl.BlockSpec(memory_space=pltpu.VMEM)
     smem = pl.BlockSpec(memory_space=pltpu.SMEM)
@@ -335,6 +340,8 @@
             block,
             block,
             pltpu.VMEM((wide, 128), F32),
+            pltpu.VMEM((rows, 2 * per_device), F32),
+            pltpu.VMEM((rows, width), BF16),
             pltpu.VMEM((peers, per_device, wide), F32),
             side,
             side,
@@ -350,7 +357,7 @@
         group_order,
         trig,
         images,
-        coil_maps,
+        jnp.swapaxes(coil_maps, 2, 3),
         measured,
         jnp.asarray(first),
         jnp.asarray(forward),

time: 70 us -> 68 us (0.971)
  local copies, waits for them, and re-layouts: 9.72 us -> 6.03 us
  Pallas kernels: 58.4 us -> 60.1 us
    unnamed x7 -> x4, local copies, waits for them, and re-layouts: 6.43 us -> 2.85 us
    pallas_call x1, Pallas kernels: 58.4 us -> 60.1 us  [fused(): pl.pallas_call(functools.partial(kernel, sizes), out_shape=jax.ShapeDtype...]
    pad x2 -> x0, local copies, waits for them, and re-layouts: 1.49 us -> none  [the longest x1 0.84 us: fused(): measured = jnp.pad(measured, ((0, rows - length), (0, 0)))]
    another operation x2 -> x0, other arithmetic: 0.82 us -> none  [fused(): jnp.stack([jnp.cos(angle), jnp.sin(angle)], axis=1)]
    cos x0 -> x1, other arithmetic: none -> 0.81 us  [fused(): trig = jnp.concatenate([jnp.cos(angle), jnp.sin(angle)], axis=0)]
    reshape x1, local copies, waits for them, and re-layouts: 0.34 us -> 1.1 us  [fused(): measured = jnp.moveaxis(kspace[0, 0], 2, 0).reshape(length, width)]
    concatenate x0 -> x1, local copies, waits for them, and re-layouts: none -> 0.75 us  [fused(): trig = jnp.concatenate([jnp.cos(angle), jnp.sin(angle)], axis=0)]
where the time goes in v3:
time: 68 us; the launch traced here: 67.8 us
  Pallas kernels  60.1 us (88%)
  local copies, waits for them, and re-layouts  6.03 us (9%)
  other arithmetic  1.61 us (2%)
    pallas_call x1, Pallas kernels, fused(): pl.pallas_call(functools.partial(kernel, sizes), out_shape=jax.ShapeDtype...  60.1 us
    unnamed x4, local copies, waits for them, and re-layouts  2.85 us

profile of v3, /device:TPU:0, one launch (start us, length us, event | category | flops | bytes accessed | tf_op | source)
XLA Modules:
  0.0 67.8 jit_solution(9184971657165760032)
XLA Ops:
  0.0 0.0 copy-start
  0.0 0.8 %convert_element_type.10 = f32[8]{0:T(128)S(1)} convert(s32[8]{0:T(128)} %param.12) | non-fusion elementwise | flops 8 | bytes 64 | tf_op jit(solution)/shard_map/convert_element_type | solution.py:29
  0.8 0.8 %fusion.1 = (f32[8,220]{1,0:T(8,128)S(1)}, f32[8,220]{1,0:T(8,128)S(1)}) fusion(f32[8,220]{1,0:T(8,128)} %param.13, f32[220]{0:T(256)S(1)} %add_convert_fusion, f32[8]{0:T(128)S(1)} %convert_element_type.10), kind=kLoop, calls=%fused_computation.3 | loop fusion | flops 5280 | bytes 22032 | tf_op jit(solution)/shard_map/cos | solution.py:322
  1.6 0.8 %copy.13 = f32[16,220]{0,1:T(8,128)} copy(f32[16,220]{1,0:T(8,128)S(1)} %pad_maximum_fusion) | data formatting | bytes 28160 | tf_op jit(solution)/shard_map/concatenate | solution.py:322
  2.4 1.3 %copy.14 = bf16[220,2,2,220]{3,2,1,0:T(2,128)(2,1)S(1)} copy(bf16[220,2,2,220]{3,2,0,1:T(2,128)(2,1)} %bitcast.7) | data formatting | bytes 774400 | tf_op jit(solution)/shard_map/transpose | solution.py:324
  3.7 1.1 %reshape.9.measured_in = bf16[220,880]{1,0:T(8,128)(2,1)} reshape(bf16[220,2,2,220]{3,2,1,0:T(2,128)(2,1)S(1)} %copy.14) | data formatting | bytes 774400 | tf_op jit(solution)/shard_map/reshape | solution.py:324
  4.8 0.0 copy-done
  4.8 1.6 %copy.15.images_ref = bf16[1,8,2,220,220]{4,3,2,1,0:T(8,128)(2,1)} copy(bf16[1,8,2,220,220]{4,2,3,1,0:T(2,128)(2,1)S(1)} %copy-done) | data formatting | bytes 3097600 | tf_op args[0]
  6.4 60.1 %shard_map.91 = f32[8,220]{1,0:T(8,128)} custom-call(s32[4]{0:T(128)} %order_ref.1, f32[220,16]{1,0:T(8,128)} %bitcast.6, bf16[1,8,2,220,220]{4,3,2,1,0:T(8,128)(2,1)} %copy.15.images_ref, bf16[2,8,220,2,220]{4,3,2,1,0:T(2,128)(2,1)} %bitcast.5, bf16[220,880]{1,0:T(8,128)(2,1)} %reshape.9.measured_in, bf16[3,224,220]{2,1,0:T(8,128)(2,1)} %constant.11.clone.first_ref, ...), custom_call_target="tpu_custom_call" | custom-call | tf_op jit(solution)/shard_map/pallas_call | solution.py:330
  66.5 1.3 %copy.17 = f32[8,220]{1,0:T(8,128)} copy(f32[8,220]{1,0:T(8,128)} %shard_map.91) | data formatting | bytes 14080
  (2 shorter events, 0.0 us)
Async XLA Ops:
  0.0 4.8 %copy-start = (bf16[1,8,2,220,220]{4,2,3,1,0:T(2,128)(2,1)S(1)}, bf16[1,8,2,220,220]{4,2,3,1,0:T(2,128)(2,1)}, u32[]{:S(2)}) copy-start(bf16[1,8,2,220,220]{4,2,3,1,0:T(2,128)(2,1)} %param.9) | copy-start | bytes 4646404
